TPU v7x, 128 devices: a whole 4x4x4 slice. The times are simulated.
128 devices in a mesh: blk: 16 (over x, z), leaf: 8 (over y, core).
Axes of the slice: x: 4, y: 4, z: 4, core: 2. Of those that a mesh axis runs over, the one named last changes fastest.
Arguments:
- columns_in: bfloat16 [16, 8, 4096, 512], P('blk', 'leaf'), may hold values from -6 to 6
- leaf_basis: bfloat16 [16, 8, 32, 128, 128], P('blk', 'leaf'), may hold values from -0.5 to 0.5
- transfers: bfloat16 [16, 8, 8, 32, 128, 256], P('blk', None, 'leaf'), may hold values from -0.4375 to 0.4375
- row_basis: bfloat16 [16, 8, 32, 128, 128], P('blk', 'leaf'), may hold values from -0.15625 to 0.15625
- ranks: int32 [16, 9, 8, 32], P('blk', None, 'leaf'), may hold values from 64 to 128, as said below
- col_owner: int32 [8], replicated, may hold values from 0 to 7, each once
- row_owner: int32 [8], replicated, may hold values from 0 to 7, each once
Outputs:
- row_sums: bfloat16 [8, 4096, 512], P('leaf', 'blk')
Inputs may be any that keep to these rules, and one draw needn't show every extreme that they name: ranks of every node of every level; the smallest and the largest value each occur. `col_owner`: each subtree number once. `row_owner`: each subtree number once.
All inputs are finite; a program needn't handle non-finite values.
Results may differ from a plain program's by a relative error of at most 0.019.
Values may be sent and summed in bfloat16 or wider, within the bound.
A program may use at most 128 MiB of HBM per device.

v0:
```python
import jax
import jax.numpy as jnp
from jax import lax
from jax.sharding import PartitionSpec as P


def apply_ranks(coeffs, live):
    row_ids = jnp.arange(coeffs.shape[-2], dtype=jnp.int32)
    keep = (row_ids[:, None] < live[..., None, None]).astype(jnp.float32)
    return coeffs * keep


def local(columns_in, leaf_basis, transfers, row_basis, ranks, col_owner, row_owner):
    owners = lax.axis_size("leaf")
    owner_bits = owners.bit_length() - 1
    blocks = lax.axis_size("blk")
    levels = transfers.shape[1]
    switch_level = levels // 2
    nodes_local = leaf_basis.shape[2]
    leaf_size = leaf_basis.shape[3]
    rank_width = leaf_basis.shape[4]
    sides = columns_in.shape[3]
    values = columns_in.reshape(nodes_local, leaf_size, sides)
    current = jnp.einsum(
        "nlr,nlh->nrh", leaf_basis[0, 0], values, preferred_element_type=jnp.float32
    )
    coeffs = apply_ranks(current, ranks[0, 0, 0]).astype(jnp.bfloat16)
    for level_index in range(1, switch_level + 1):
        half_j = 2 ** (levels - level_index - owner_bits)
        half_i = 2 ** (level_index - 1)
        previous = coeffs.reshape(half_j, 2, half_i, rank_width, sides)
        mixing = transfers[0, level_index - 1, 0].reshape(
            half_j, half_i, 2, rank_width, 2, rank_width
        )
        live = ranks[0, level_index, 0]
        if level_index < switch_level:
            current = jnp.einsum(
                "jibrtq,jtiqh->jibrh", mixing, previous, preferred_element_type=jnp.float32
            )
        else:
            current = jnp.einsum(
                "jibrtq,jtiqh->ibjrh", mixing, previous, preferred_element_type=jnp.float32
            )
            live = live.reshape(half_j, half_i, 2).transpose(1, 2, 0)
        coeffs = apply_ranks(
            current.reshape(nodes_local, rank_width, sides), live.reshape(nodes_local)
        ).astype(jnp.bfloat16)
    sub_i = 2 ** (switch_level - owner_bits)
    part_j = 2 ** (levels - switch_level - owner_bits)
    grouped = coeffs.reshape(owners, sub_i, part_j, rank_width, sides)
    outgoing = jnp.take(grouped, row_owner, axis=0)
    incoming = lax.all_to_all(outgoing, "leaf", split_axis=0, concat_axis=2, tiled=True)
    incoming = incoming.reshape(sub_i, owners, part_j, rank_width, sides)
    inverse = jnp.argsort(col_owner)
    coeffs = jnp.take(incoming, inverse, axis=1).reshape(nodes_local, rank_width, sides)
    for level_index in range(switch_level + 1, levels + 1):
        half_i = 2 ** (level_index - 1 - owner_bits)
        half_j = 2 ** (levels - level_index)
        previous = coeffs.reshape(half_i, half_j, 2, rank_width, sides)
        mixing = transfers[0, level_index - 1, 0].reshape(
            half_i, 2, half_j, rank_width, 2, rank_width
        )
        current = jnp.einsum(
            "ibjrtq,ijtqh->ibjrh", mixing, previous, preferred_element_type=jnp.float32
        )
        coeffs = apply_ranks(
            current.reshape(nodes_local, rank_width, sides), ranks[0, level_index, 0]
        ).astype(jnp.bfloat16)
    sub_rows = nodes_local * leaf_size
    share = sub_rows // blocks
    row_flat = row_basis[0, 0].reshape(sub_rows, rank_width)
    basis = row_flat.reshape(share * lax.axis_size("blk") // leaf_size, leaf_size, rank_width)
    result = jnp.einsum("nlr,nrh->nlh", basis, coeffs, preferred_element_type=jnp.float32)
    summed = lax.psum_scatter(
        result.reshape(share * lax.axis_size("blk"), sides).astype(jnp.bfloat16),
        "blk",
        scatter_dimension=0,
        tiled=True,
    ).astype(jnp.float32)
    return summed.reshape(1, share, sides).astype(jnp.bfloat16)


def solution(mesh):
    return jax.shard_map(
        local,
        mesh=mesh,
        in_specs=(
            P("blk", "leaf", None, None),
            P("blk", "leaf", None, None, None),
            P("blk", None, "leaf", None, None, None),
            P("blk", "leaf", None, None, None),
            P("blk", None, "leaf", None),
            P(),
            P(),
        ),
        out_specs=P("leaf", "blk", None),
        check_vma=False,
    )
```

profile of v0, /device:TPU:0, one launch (start us, length us, event | category | flops | bytes accessed | tf_op | source)
XLA Modules:
  0.0 280.4 jit_solution(11047903549985685326)
XLA Ops:
  8.8 11.4 %fusion.51 = (bf16[1,1,1,32,128,256]{5,4,3,2,1,0:T(8,128)(2,1)}, bf16[1,1,1,32,128,256]{5,4,3,2,1,0:T(8,128)(2,1)}, bf16[1,1,1,32,128,256]{5,4,3,2,1,0:T(8,128)(...) fusion(bf16[1,8,1,32,128,256]{5,4,3,2,1,0:T(8,128)(2,1)} %param.9), kind=kLoop, calls=%fused_computation.75 | loop fusion | bytes 33554432 | tf_op jit(solution)/shard_map/slice | solution.py:60
  23.4 3.2 %copy.92 = bf16[1,1,1,32,128,256]{4,5,3,2,1,0:T(8,128)(2,1)S(1)} copy(bf16[1,1,1,32,128,256]{5,4,3,2,1,0:T(8,128)(2,1)} %get-tuple-element.19) | data formatting | bytes 4194304
  26.9 4.1 %copy.93 = bf16[1,1,1,32,128,256]{4,5,3,2,1,0:T(8,128)(2,1)} copy(bf16[1,1,1,32,128,256]{5,4,3,2,1,0:T(8,128)(2,1)} %get-tuple-element.18) | data formatting | bytes 4194304
  31.4 4.1 %copy.94 = bf16[1,1,1,32,128,256]{4,5,3,2,1,0:T(8,128)(2,1)} copy(bf16[1,1,1,32,128,256]{5,4,3,2,1,0:T(8,128)(2,1)} %get-tuple-element.17) | data formatting | bytes 4194304
  35.6 3.7 %multiply_convert_fusion.3 = bf16[32,128,512]{2,1,0:T(8,128)(2,1)S(1)} fusion(f32[32,128]{1,0:T(8,128)S(1)} %get-tuple-element.31, bf16[32,128,512]{2,1,0:T(8,128)(2,1)} %bitcast.151, bf16[1,1,32,128,128]{4,3,2,1,0:T(8,128)(2,1)S(1)} %copy-done), kind=kOutput, calls=%fused_computation.15 | convolution fusion | flops 541065216 | bytes 9453568 | tf_op jit(solution)/shard_map/nlr,nlh->nrh/dot_general | solution.py:24
  45.1 3.2 %fusion = bf16[8,2,2,128,512]{3,4,1,2,0:T(8,128)(2,1)} fusion(f32[8,2,2,128]{3,1,2,0:T(2,128)S(1)} %compare_convert_fusion.3, f32[2,2,8,128,512]{3,4,2,1,0:T(8,128)S(1)} %bitcast.138, f32[2,2,8,128]{3,1,0,2:T(2,128)S(1)} %compare_convert_fusion.4, bf16[2,8,2,128,2,128]{3,5,4,2,1,0:T(8,128)(2,1)S(1)} %bitcast.146), kind=kOutput, calls=%fused_computation.3 | convolution fusion | flops 1082130432 | bytes 14712832 | tf_op jit(solution)/shard_map/jibrtq,jtiqh->ibjrh/dot_general | solution.py:41
  48.4 5.2 %gather_fusion = bf16[8,2,2,128,512]{3,4,1,2,0:T(8,128)(2,1)} fusion(bf16[8,2,2,128,512]{3,4,1,2,0:T(8,128)(2,1)} %fusion, s32[1024]{0:T(1024)S(1)} %pad_clamp_fusion.1), kind=kCustom, calls=%fused_computation | custom fusion | bytes 8388640 | tf_op jit(solution)/shard_map/jit(_take)/gather | solution.py:51
  53.6 4.6 %broadcast_select_fusion = bf16[8,2,2,128,512]{3,4,1,2,0:T(8,128)(2,1)} fusion(bf16[8,2,2,128,512]{3,4,1,2,0:T(8,128)(2,1)} %gather_fusion, pred[8]{0:T(512)(128)(4,1)S(1)} %compare_and_fusion), kind=kLoop, calls=%fused_computation.38 | loop fusion | flops 2097152 | bytes 8388616 | tf_op jit(solution)/shard_map/jit(_take)/select_n | solution.py:51
  58.2 4.7 %all-to-all-start = ((bf16[8,2,2,128,512]{3,4,1,2,0:T(8,128)(2,1)}), bf16[8,2,2,128,512]{3,4,1,2,0:T(8,128)(2,1)}, u32[]{:S(2)}, u32[]{:S(2)}) async-start(bf16[8,2,2,128,512]{3,4,1,2,0:T(8,128)(2,1)} %broadcast_select_fusion), calls=%async_computation | async-start | bytes 8388608 | tf_op jit(solution)/shard_map/all_to_all | solution.py:52
  66.2 4.2 %copy.96 = bf16[1,1,1,32,128,256]{4,5,3,2,1,0:T(8,128)(2,1)} copy(bf16[1,1,1,32,128,256]{5,4,3,2,1,0:T(8,128)(2,1)} %get-tuple-element.15) | data formatting | bytes 4194304
  70.5 4.1 %copy.97 = bf16[1,1,1,32,128,256]{4,5,3,2,1,0:T(8,128)(2,1)} copy(bf16[1,1,1,32,128,256]{5,4,3,2,1,0:T(8,128)(2,1)} %get-tuple-element.14) | data formatting | bytes 4194304
  78.9 33.8 %all-to-all-done = bf16[8,2,2,128,512]{3,4,1,2,0:T(8,128)(2,1)} async-done(((bf16[8,2,2,128,512]{3,4,1,2,0:T(8,128)(2,1)}), bf16[8,2,2,128,512]{3,4,1,2,0:T(8,128)(2,1)}, u32[]{:S(2)}, u32[]{:S(2)}) %all-to-all-start) | async-done | bytes 4194336 | tf_op jit(solution)/shard_map/all_to_all | solution.py:52
  112.7 5.4 %gather_fusion.1 = bf16[8,2,2,128,512]{3,4,1,2,0:T(8,128)(2,1)} fusion(bf16[2,8,2,128,512]{3,4,0,2,1:T(8,128)(2,1)} %bitcast.33, s32[1024]{0:T(1024)S(1)} %pad_clamp_fusion), kind=kCustom, calls=%fused_computation.1 | custom fusion | bytes 8388640 | tf_op jit(solution)/shard_map/jit(_take)/gather | solution.py:55
  118.1 6.7 %fusion.31 = f32[2,2,8,128,512]{3,4,1,2,0:T(8,128)} fusion(bf16[2,2,8,128,2,128]{3,5,4,2,1,0:T(8,128)(2,1)S(1)} %bitcast.149, bf16[8,2,2,128,512]{3,4,1,2,0:T(8,128)(2,1)} %gather_fusion.1, pred[8]{0:T(512)(128)(4,1)S(1)} %compare_and_fusion.1), kind=kOutput, calls=%fused_computation.39 | convolution fusion | flops 1075838976 | bytes 14680072 | tf_op jit(solution)/shard_map/ibjrtq,ijtqh->ibjrh/dot_general | solution.py:63
  124.8 8.9 %copy.39 = f32[2,2,8,128,512]{4,3,2,1,0:T(8,128)} copy(f32[2,2,8,128,512]{3,4,1,2,0:T(8,128)} %fusion.31) | data formatting | bytes 16777216 | tf_op jit(solution)/shard_map/ibjrtq,ijtqh->ibjrh/transpose | solution.py:63
  133.7 8.5 %fusion.37 = f32[4,2,4,128,512]{3,4,1,2,0:T(8,128)} fusion(f32[4,4,2,128,512]{4,3,2,1,0:T(8,128)} %bitcast.139, f32[4,4,2,128]{3,2,1,0:T(2,128)S(1)} %compare_convert_fusion.2, bf16[4,2,4,128,2,128]{3,5,4,2,1,0:T(8,128)(2,1)S(1)} %bitcast.148), kind=kOutput, calls=%fused_computation.41 | convolution fusion | flops 1077936128 | bytes 18890752 | tf_op jit(solution)/shard_map/ibjrtq,ijtqh->ibjrh/dot_general | solution.py:63
  142.2 10.1 %copy.43 = f32[4,2,4,128,512]{4,3,2,1,0:T(8,128)} copy(f32[4,2,4,128,512]{3,4,1,2,0:T(8,128)} %fusion.37) | data formatting | bytes 16777216 | tf_op jit(solution)/shard_map/ibjrtq,ijtqh->ibjrh/transpose | solution.py:63
  152.3 8.5 %fusion.34 = f32[8,2,2,128,512]{3,4,1,2,0:T(8,128)} fusion(f32[8,2,2,128,512]{4,3,2,1,0:T(8,128)} %bitcast.140, f32[8,2,2,128]{3,2,1,0:T(2,128)S(1)} %compare_convert_fusion.1, bf16[8,2,2,128,2,128]{3,5,4,2,1,0:T(8,128)(2,1)S(1)} %bitcast.147), kind=kOutput, calls=%fused_computation.40 | convolution fusion | flops 1077936128 | bytes 18890752 | tf_op jit(solution)/shard_map/ibjrtq,ijtqh->ibjrh/dot_general | solution.py:63
  160.8 9.1 %copy.47 = f32[8,2,2,128,512]{4,3,2,1,0:T(8,128)} copy(f32[8,2,2,128,512]{3,4,1,2,0:T(8,128)} %fusion.34) | data formatting | bytes 16777216 | tf_op jit(solution)/shard_map/ibjrtq,ijtqh->ibjrh/transpose | solution.py:63
  169.9 4.0 %fusion.1 = bf16[16,2,128,512]{3,2,1,0:T(8,128)(2,1)S(1)} fusion(f32[8,2,2,128,512]{4,3,2,1,0:T(8,128)} %copy.47, f32[16,2,128]{2,1,0:T(2,128)S(1)} %compare_convert_fusion), kind=kLoop, calls=%fused_computation.5 | loop fusion | flops 4194304 | bytes 12599296 | tf_op jit(solution)/shard_map/convert_element_type | solution.py:68
  174.0 4.6 %fusion.21 = f32[16,512,2,128,1]{3,1,4,2,0:T(8,128)} fusion(bf16[16,2,128,2,128]{2,4,3,1,0:T(8,128)(2,1)S(1)} %bitcast.144, bf16[16,2,128,512]{3,2,1,0:T(8,128)(2,1)S(1)} %fusion.1), kind=kOutput, calls=%fused_computation.27 | convolution fusion | flops 1073741824 | bytes 14680064 | tf_op jit(solution)/shard_map/ibjrtq,ijtqh->ibjrh/dot_general | solution.py:63
  178.6 9.1 %copy.51 = f32[32,128,512]{2,1,0:T(8,128)} copy(f32[32,128,512]{1,2,0:T(8,128)} %bitcast.137) | data formatting | bytes 16777216 | tf_op jit(solution)/shard_map/reshape | solution.py:67
  187.7 6.8 %fusion.42 = bf16[32,512,128]{1,2,0:T(8,128)(2,1)} fusion(f32[32,128,512]{2,1,0:T(8,128)} %copy.51, f32[32,128]{1,0:T(8,128)S(1)} %get-tuple-element.32, bf16[1,1,32,128,128]{4,3,2,1,0:T(8,128)(2,1)S(1)} %copy-done.10), kind=kOutput, calls=%fused_computation.42 | convolution fusion | flops 543162368 | bytes 13647872 | tf_op jit(solution)/shard_map/nlr,nrh->nlh/dot_general | solution.py:73
  194.5 79.1 %reduce-scatter.2.cloned.1.call-done = bf16[256,512]{1,0:T(8,128)(2,1)} async-done(((bf16[4096,512]{1,0:T(8,128)(2,1)}), bf16[256,512]{1,0:T(8,128)(2,1)}) %reduce-scatter.2.cloned.1.call-update) | async-done | bytes 262160 | tf_op jit(solution)/shard_map/reduce_scatter | solution.py:74
  (60 shorter events, 19.6 us)
Async XLA Ops:
  6.5 29.1 %copy-start = (bf16[1,1,32,128,128]{4,3,2,1,0:T(8,128)(2,1)S(1)}, bf16[1,1,32,128,128]{4,3,2,1,0:T(8,128)(2,1)}, u32[]{:S(2)}) copy-start(bf16[1,1,32,128,128]{4,3,2,1,0:T(8,128)(2,1)} %param.8) | copy-start | bytes 3145732
  35.6 3.7 %copy-start.5 = (bf16[1,1,1,32,128,256]{4,5,3,2,1,0:T(8,128)(2,1)S(1)}, bf16[1,1,1,32,128,256]{4,5,3,2,1,0:T(8,128)(2,1)}, u32[]{:S(2)}) copy-start(bf16[1,1,1,32,128,256]{4,5,3,2,1,0:T(8,128)(2,1)} %copy.91) | copy-start | bytes 6291460
  42.1 3.1 %copy-start.6 = (bf16[1,1,1,32,128,256]{4,5,3,2,1,0:T(8,128)(2,1)S(1)}, bf16[1,1,1,32,128,256]{4,5,3,2,1,0:T(8,128)(2,1)}, u32[]{:S(2)}) copy-start(bf16[1,1,1,32,128,256]{4,5,3,2,1,0:T(8,128)(2,1)} %copy.94) | copy-start | bytes 6291460
  58.2 4.9 %copy-start.3 = (bf16[1,1,1,32,128,256]{5,4,3,2,1,0:T(8,128)(2,1)S(1)}, bf16[1,1,1,32,128,256]{5,4,3,2,1,0:T(8,128)(2,1)}, u32[]{:S(2)}) copy-start(bf16[1,1,1,32,128,256]{5,4,3,2,1,0:T(8,128)(2,1)} %get-tuple-element.16) | copy-start | bytes 6291460
  58.2 54.5 %all-to-all-start = ((bf16[8,2,2,128,512]{3,4,1,2,0:T(8,128)(2,1)}), bf16[8,2,2,128,512]{3,4,1,2,0:T(8,128)(2,1)}, u32[]{:S(2)}, u32[]{:S(2)}) async-start(bf16[8,2,2,128,512]{3,4,1,2,0:T(8,128)(2,1)} %broadcast_select_fusion), calls=%async_computation | async-start | bytes 8388608 | tf_op jit(solution)/shard_map/all_to_all | solution.py:52
  63.0 210.6 %reduce-scatter.2.cloned.1.call-start = ((), (), s32[]{:S(2)}) async-start(), calls=%async_computation.2 | async-start | bytes 4456448 | tf_op jit(solution)/shard_map/reduce_scatter | solution.py:74
  66.2 8.5 %copy-start.2 = (bf16[1,1,1,32,128,256]{5,4,3,2,1,0:T(8,128)(2,1)S(1)}, bf16[1,1,1,32,128,256]{5,4,3,2,1,0:T(8,128)(2,1)}, u32[]{:S(2)}) copy-start(bf16[1,1,1,32,128,256]{5,4,3,2,1,0:T(8,128)(2,1)} %get-tuple-element.21) | copy-start | bytes 6291460
  70.5 7.1 %copy-start.11 = (s32[8]{0:T(128)S(1)}, s32[8]{0:T(128)}, u32[]{:S(2)}) copy-start(s32[8]{0:T(128)} %param.12) | copy-start | bytes 100
  112.7 5.4 %copy-start.9 = (bf16[1,1,1,32,128,256]{4,5,3,2,1,0:T(8,128)(2,1)S(1)}, bf16[1,1,1,32,128,256]{4,5,3,2,1,0:T(8,128)(2,1)}, u32[]{:S(2)}) copy-start(bf16[1,1,1,32,128,256]{4,5,3,2,1,0:T(8,128)(2,1)} %copy.95) | copy-start | bytes 6291460
  124.8 8.9 %copy-start.8 = (bf16[1,1,1,32,128,256]{4,5,3,2,1,0:T(8,128)(2,1)S(1)}, bf16[1,1,1,32,128,256]{4,5,3,2,1,0:T(8,128)(2,1)}, u32[]{:S(2)}) copy-start(bf16[1,1,1,32,128,256]{4,5,3,2,1,0:T(8,128)(2,1)} %copy.96) | copy-start | bytes 6291460
  142.2 10.1 %copy-start.7 = (bf16[1,1,1,32,128,256]{4,5,3,2,1,0:T(8,128)(2,1)S(1)}, bf16[1,1,1,32,128,256]{4,5,3,2,1,0:T(8,128)(2,1)}, u32[]{:S(2)}) copy-start(bf16[1,1,1,32,128,256]{4,5,3,2,1,0:T(8,128)(2,1)} %copy.97) | copy-start | bytes 6291460
  169.9 4.0 %copy-start.4 = (bf16[1,1,1,32,128,256]{4,5,3,2,1,0:T(8,128)(2,1)S(1)}, bf16[1,1,1,32,128,256]{4,5,3,2,1,0:T(8,128)(2,1)}, u32[]{:S(2)}) copy-start(bf16[1,1,1,32,128,256]{4,5,3,2,1,0:T(8,128)(2,1)} %copy.98) | copy-start | bytes 6291460
  178.6 9.1 %copy-start.10 = (bf16[1,1,32,128,128]{4,3,2,1,0:T(8,128)(2,1)S(1)}, bf16[1,1,32,128,128]{4,3,2,1,0:T(8,128)(2,1)}, u32[]{:S(2)}) copy-start(bf16[1,1,32,128,128]{4,3,2,1,0:T(8,128)(2,1)} %param.10) | copy-start | bytes 3145732
  187.7 85.9 %copy-start.1 = (bf16[1,1,32,128,128]{4,3,2,1,0:T(8,128)(2,1)S(1)}, bf16[1,1,32,128,128]{4,3,2,1,0:T(8,128)(2,1)}, u32[]{:S(2)}) copy-start(bf16[1,1,32,128,128]{4,3,2,1,0:T(8,128)(2,1)} %param.8) | copy-start | bytes 3145732
Sparse Core Ops, SparseCore 0:
  194.6 78.9 reduce-scatter.1
where the time goes:
time: 282 us; the launch traced here: 280 us
  waiting for transfers between devices  113 us (40%)
  local copies, waits for them, and re-layouts  89.4 us (32%)
  matrix products  47.9 us (17%)
  between operations  13.6 us (5%)
  other arithmetic  11.6 us (4%)
  starting transfers between devices  4.93 us (2%)
    reduce_scatter x1, waiting for transfers between devices, local(): lax.psum_scatter(result.reshape(share * lax.axis_size('blk'), sides).asty...  79.1 us
    all_to_all x1, waiting for transfers between devices, local(): lax.all_to_all(outgoing, 'leaf', split_axis=0, concat_axis=2, tiled=True)  33.8 us
    unnamed x32, local copies, waits for them, and re-layouts  28.5 us
    dot_general x4, matrix products, local(): jnp.einsum('ibjrtq,ijtqh->ibjrh', mixing, previous, preferred_element_typ...  28.4 us
    transpose x3, local copies, waits for them, and re-layouts, local(): jnp.einsum('ibjrtq,ijtqh->ibjrh', mixing, previous, preferred_element_typ...  28 us
    slice x1, local copies, waits for them, and re-layouts, local(): transfers[0, level_index - 1, 0]  11.4 us
    reshape x1, local copies, waits for them, and re-layouts, local(): current.reshape(nodes_local, rank_width, sides)  9.1 us
    dot_general x1, matrix products, local(): jnp.einsum('nlr,nrh->nlh', basis, coeffs, preferred_element_type=jnp.floa...  6.77 us
  transfers between devices with their start and end apart: 2, of which 2 were waited for; matrix products, arithmetic and copies ran while one was open for 6% of the time, Pallas kernels for 0%

commit v1 on v0

v1 whole, which is shorter than its diff:
```python
import functools

import jax
import jax.numpy as jnp
from jax import lax
from jax.experimental import pallas as pl
from jax.experimental.pallas import tpu as pltpu
from jax.sharding import PartitionSpec as P

MESH = pl.DeviceIdType.MESH
SIDE = 4
PEERS = (4, 3, 5, 2, 6, 1, 7)
QUARTERS = (2, 1, 3, 0)


def dot(a, b):
    return jnp.dot(a, b, preferred_element_type=jnp.float32)


def kernel(
    chunks, width, rank,
    x_hbm, leaf_hbm, mix_hbm, row_hbm, ranks, col_owner, row_owner,
    out,
    xv, leaf, t1, t2, t3, t4, t5, t6, t7, t8, row,
    ca, cb, send, recv, c5, c6, c7, c8,
    xs, zs, xr, zr, xs2, zs2, xr2, zr2,
    in_sem, x_sem,
    a_send, a_recv, xs_sem, xr_sem, zs_sem, zr_sem, xs2_sem, xr2_sem, zs2_sem, zr2_sem,
):
    mixes = (t1, t2, t3, t4, t5, t6, t7, t8)
    me = lax.axis_index("leaf")
    blk = lax.axis_index("blk")
    bx, bz = lax.div(blk, SIDE), lax.rem(blk, SIDE)

    def leaf_peer(d):
        return {"blk": blk, "leaf": lax.rem(me + d, 8)}

    def x_peer(d):
        return {"blk": lax.rem(bx + d, SIDE) * SIDE + bz, "leaf": me}

    def z_peer(d):
        return {"blk": bx * SIDE + lax.rem(bz + d, SIDE), "leaf": me}

    def x_in(c):
        return pltpu.make_async_copy(
            x_hbm.at[:, :, pl.ds(pl.multiple_of(c * width, width), width)],
            xv.at[c], x_sem.at[c])

    def weight_in(i):
        if i == 0:
            return pltpu.make_async_copy(leaf_hbm, leaf, in_sem.at[0])
        if i == 9:
            return pltpu.make_async_copy(row_hbm, row, in_sem.at[9])
        return pltpu.make_async_copy(mix_hbm.at[i - 1], mixes[i - 1], in_sem.at[i])

    weight_in(0).start()
    x_in(0).start()
    for i in range(1, 5):
        weight_in(i).start()
    for c in range(1, chunks):
        x_in(c).start()
    for i in range(5, 10):
        weight_in(i).start()

    barrier = pltpu.get_barrier_semaphore()
    for d in range(1, 8):
        pl.semaphore_signal(barrier, inc=1, device_id=leaf_peer(d), device_id_type=MESH)
    for d in range(1, SIDE):
        pl.semaphore_signal(barrier, inc=1, device_id=x_peer(d), device_id_type=MESH)
        pl.semaphore_signal(barrier, inc=1, device_id=z_peer(d), device_id_type=MESH)

    row_ids = lax.broadcasted_iota(jnp.int32, (rank, width), 0)

    def keep(value, live):
        return jnp.where(row_ids < live, value, 0.0).astype(jnp.bfloat16)

    def mix(lhs, top, bottom):
        return dot(lhs, jnp.concatenate([top, bottom], axis=0))

    def pair(ref, p):
        return ref[pl.ds(2 * p, 2)].reshape(2 * rank, 2 * rank)

    def leaf_level(c):
        @pl.loop(0, 8)
        def _(g):
            for u in range(4):
                n = 4 * g + u
                value = lax.dot_general(
                    leaf[n], xv[c, n], (((0,), (0,)), ((), ())),
                    preferred_element_type=jnp.float32)
                ca[n] = keep(value, ranks[0, n])

    def column_level(level, source, target):
        half_i = 2 ** (level - 1)

        @pl.loop(0, 4)
        def _(g):
            for u in range(4):
                p = 4 * g + u
                a = (p // half_i) * (2 * half_i) + p % half_i
                value = mix(pair(mixes[level - 1], p), source[a], source[a + half_i])
                target[2 * p] = keep(value[:rank], ranks[level, 2 * p])
                target[2 * p + 1] = keep(value[rank:], ranks[level, 2 * p + 1])

    def a2a(c, d):
        return pltpu.make_async_remote_copy(
            src_ref=send.at[c, d], dst_ref=recv.at[c, d - 1],
            send_sem=a_send.at[c, d - 1], recv_sem=a_recv.at[c, d - 1],
            device_id=leaf_peer(d), device_id_type=MESH)

    def switch_level(c, source):
        waiting = None
        for d in PEERS + (0,):
            s = row_owner[lax.rem(me + d, 8)]
            for j in range(2):
                node = j * 8 + s
                value = mix(pair(t4, node), source[2 * j * 8 + s], source[(2 * j + 1) * 8 + s])
                send[c, d, j] = keep(value[:rank], ranks[4, 2 * node])
                send[c, d, 2 + j] = keep(value[rank:], ranks[4, 2 * node + 1])
            if waiting is not None:
                a2a(c, waiting).start()
            waiting = d

    def phase_a(c):
        x_in(c).wait()

        @pl.when(c == 0)
        def _():
            weight_in(0).wait()

        leaf_level(c)
        for level, source, target in ((1, ca, cb), (2, cb, ca), (3, ca, cb)):
            @pl.when(c == 0)
            def _():
                weight_in(level).wait()

            column_level(level, source, target)

        @pl.when(c == 0)
        def _():
            weight_in(4).wait()
            pl.semaphore_wait(barrier, 7 + 2 * (SIDE - 1))

        switch_level(c, cb)

    def x_first(c, d):
        return pltpu.make_async_remote_copy(
            src_ref=xs.at[c, d], dst_ref=xr.at[c, d - 1],
            send_sem=xs_sem.at[c, d - 1], recv_sem=xr_sem.at[c, d - 1],
            device_id=x_peer(d), device_id_type=MESH)

    def z_first(c, d):
        return pltpu.make_async_remote_copy(
            src_ref=zs.at[c, d], dst_ref=zr.at[c, d - 1],
            send_sem=zs_sem.at[c, d - 1], recv_sem=zr_sem.at[c, d - 1],
            device_id=z_peer(d), device_id_type=MESH)

    def z_second(c, d):
        return pltpu.make_async_remote_copy(
            src_ref=zs2.at[c, d], dst_ref=zr2.at[c, d - 1],
            send_sem=zs2_sem.at[c, d - 1], recv_sem=zr2_sem.at[c, d - 1],
            device_id=z_peer(d), device_id_type=MESH)

    def x_second(c, d):
        return pltpu.make_async_remote_copy(
            src_ref=xs2.at[c, d], dst_ref=xr2.at[c, d - 1],
            send_sem=xs2_sem.at[c, d - 1], recv_sem=xr2_sem.at[c, d - 1],
            device_id=x_peer(d), device_id_type=MESH)

    def arrive(c, d):
        owner = lax.rem(me + 8 - d, 8)
        j = col_owner[owner]
        for i in range(2):
            lhs = jnp.concatenate([t5[2 * i * 8 + j], t5[(2 * i + 1) * 8 + j]], axis=0)
            if d == 0:
                nodes = send[c, 0, pl.ds(2 * i, 2)]
            else:
                nodes = recv[c, d - 1, pl.ds(2 * i, 2)]
            value = dot(lhs, nodes.reshape(2 * rank, width))
            for e in range(2):
                c5[2 * i + e, d] = keep(
                    value[e * rank:(e + 1) * rank], ranks[5, (2 * i + e) * 8 + j])

    def quarter(c, dq, places):
        q = lax.rem(bx + dq, SIDE)
        for j in range(4):
            lhs = jnp.concatenate([t6[2 * q * 4 + j], t6[(2 * q + 1) * 4 + j]], axis=0)
            value = mix(lhs, c5[q, places[2 * j]], c5[q, places[2 * j + 1]])
            for e in range(2):
                c6[e * 4 + j] = keep(
                    value[e * rank:(e + 1) * rank], ranks[6, (2 * q + e) * 4 + j])
        for i in range(2):
            for j in range(2):
                base = (2 * q + i) * 4 + j
                lhs = jnp.concatenate([t7[base], t7[base + 2]], axis=0)
                value = mix(lhs, c6[i * 4 + 2 * j], c6[i * 4 + 2 * j + 1])
                for e in range(2):
                    c7[(i * 2 + e) * 2 + j] = keep(
                        value[e * rank:(e + 1) * rank], ranks[7, base + 2 * e])
        for i in range(4):
            node = 4 * q + i
            value = mix(pair(t8, node), c7[2 * i], c7[2 * i + 1])
            for e in range(2):
                c8[2 * i + e] = keep(
                    value[e * rank:(e + 1) * rank], ranks[8, 2 * node + e])
        for m in range(4):
            xs[c, dq, m] = dot(row[8 * q + 2 * m], c8[2 * m]).astype(jnp.bfloat16)
        for r in range(SIDE):
            m = lax.rem(bz + r, SIDE)
            zs[c, r, dq] = dot(row[8 * q + 2 * m + 1], c8[2 * m + 1]).astype(jnp.bfloat16)

    def phase_b(c):
        @pl.when(c == 0)
        def _():
            for i in range(5, 10):
                weight_in(i).wait()

        arrive(c, 0)
        for d in (7, 1, 6, 2, 5, 3, 4):
            a2a(c, d).wait_recv()
            arrive(c, d)
        places = []
        for wanted in range(8):
            found = jnp.int32(0)
            for o in range(8):
                found = found + jnp.where(col_owner[o] == wanted, o, 0)
            places.append(lax.rem(me + 32 - found, 8))
        for index, dq in enumerate(QUARTERS):
            quarter(c, dq, places)
            if index:
                x_first(c, QUARTERS[index - 1]).start()
        for d in (2, 1, 3):
            z_first(c, d).start()

    def wide(value):
        return value.astype(jnp.float32)

    def first_sum(c):
        for d in (2, 1, 3):
            x_first(c, d).wait_recv()
        for r in (2, 1, 3, 0):
            m = lax.rem(bz + r, SIDE)
            total = wide(xs[c, 0, m])
            for d in range(SIDE - 1):
                total = total + wide(xr[c, d, m])
            zs2[c, r] = total.astype(jnp.bfloat16)
        for d in (2, 1, 3):
            z_second(c, d).start()
        for d in (2, 1, 3):
            z_first(c, d).wait_recv()
        for r in (2, 1, 3, 0):
            total = wide(zs[c, 0, r])
            for d in range(SIDE - 1):
                total = total + wide(zr[c, d, r])
            xs2[c, r] = total.astype(jnp.bfloat16)
        for d in (2, 1, 3):
            x_second(c, d).start()

    def last_sum(c):
        columns = pl.ds(pl.multiple_of(c * width, width), width)
        for d in (1, 3, 2):
            z_second(c, d).wait_recv()
        total = wide(zs2[c, 0])
        for d in range(SIDE - 1):
            total = total + wide(zr2[c, d])
        out[pl.ds(0, rank), columns] = total.astype(jnp.bfloat16)
        for d in (1, 3, 2):
            x_second(c, d).wait_recv()
        total = wide(xs2[c, 0])
        for d in range(SIDE - 1):
            total = total + wide(xr2[c, d])
        out[pl.ds(rank, rank), columns] = total.astype(jnp.bfloat16)

    @pl.loop(0, chunks)
    def _(c):
        phase_a(c)

    @pl.loop(0, chunks)
    def _(c):
        @pl.when(c >= 1)
        def _():
            first_sum(c - 1)

        phase_b(c)

        @pl.when(c >= 1)
        def _():
            last_sum(c - 1)

    first_sum(chunks - 1)
    last_sum(chunks - 1)

    @pl.loop(0, chunks)
    def _(c):
        for d in range(1, 8):
            a2a(c, d).wait_send()
        for d in range(1, SIDE):
            x_first(c, d).wait_send()
            z_first(c, d).wait_send()
            x_second(c, d).wait_send()
            z_second(c, d).wait_send()


def local(columns_in, leaf_basis, transfers, row_basis, ranks, col_owner, row_owner):
    nodes, leaf_size, rank = leaf_basis.shape[2:]
    sides = columns_in.shape[3]
    levels = transfers.shape[1]
    width = 128
    chunks = sides // width
    bf = jnp.bfloat16
    dma = pltpu.SemaphoreType.DMA
    hbm = pl.BlockSpec(memory_space=pltpu.HBM)
    smem = pl.BlockSpec(memory_space=pltpu.SMEM)
    tile = (rank, width)
    scratch = [pltpu.VMEM((chunks, nodes, leaf_size, width), bf), pltpu.VMEM((nodes, leaf_size, rank), bf)]
    scratch += [pltpu.VMEM((nodes, rank, 2 * rank), bf)] * levels
    scratch += [pltpu.VMEM((nodes, leaf_size, rank), bf)]
    scratch += [pltpu.VMEM((nodes,) + tile, bf)] * 2
    scratch += [pltpu.VMEM((chunks, 8, 4) + tile, bf), pltpu.VMEM((chunks, 7, 4) + tile, bf)]
    scratch += [pltpu.VMEM((4, 8) + tile, bf)] + [pltpu.VMEM((8,) + tile, bf)] * 3
    scratch += [pltpu.VMEM((chunks, 4, 4) + tile, bf)] * 2
    scratch += [pltpu.VMEM((chunks, 3, 4) + tile, bf)] * 2
    scratch += [pltpu.VMEM((chunks, 4) + tile, bf)] * 2
    scratch += [pltpu.VMEM((chunks, 3) + tile, bf)] * 2
    scratch += [dma((10,)), dma((chunks,)), dma((chunks, 7)), dma((chunks, 7))]
    scratch += [dma((chunks, 3))] * 8
    share = nodes * leaf_size // lax.axis_size("blk")
    result = pl.pallas_call(
        functools.partial(kernel, chunks, width, rank),
        out_shape=jax.ShapeDtypeStruct((share, sides), bf),
        in_specs=[hbm] * 4 + [smem] * 3,
        out_specs=pl.BlockSpec(memory_space=pltpu.VMEM),
        scratch_shapes=scratch,
        compiler_params=pltpu.CompilerParams(
            collective_id=0, has_side_effects=True, vmem_limit_bytes=60 * 1024 * 1024),
        name="block_row",
    )(
        columns_in.reshape(nodes, leaf_size, sides),
        leaf_basis[0, 0],
        transfers[0, :, 0],
        row_basis[0, 0],
        ranks[0, :, 0],
        col_owner,
        row_owner,
    )
    return result.reshape(1, share, sides)


def solution(mesh):
    return jax.shard_map(
        local,
        mesh=mesh,
        in_specs=(
            P("blk", "leaf", None, None),
            P("blk", "leaf", None, None, None),
            P("blk", None, "leaf", None, None, None),
            P("blk", "leaf", None, None, None),
            P("blk", None, "leaf", None),
            P(),
            P(),
        ),
        out_specs=P("leaf", "blk", None),
        check_vma=False,
    )
```

time: 282 us -> 97.5 us (0.35)
  waiting for transfers between devices: 113 us -> 0 us
  Pallas kernels: 0 us -> 94.4 us
  local copies, waits for them, and re-layouts: 89.4 us -> 2.96 us
  matrix products: 47.9 us -> 0 us
  between operations: 13.6 us -> 0.01 us
  other arithmetic: 11.6 us -> 0 us
  starting transfers between devices: 4.93 us -> 0 us
    pallas_call x0 -> x1, Pallas kernels: none -> 94.4 us  [local(): pl.pallas_call(functools.partial(kernel, chunks, width, rank), out_shape=...]
    reduce_scatter x1 -> x0, waiting for transfers between devices: 79.1 us -> none  [local(): lax.psum_scatter(result.reshape(share * lax.axis_size('blk'), sides).asty...]
    dot_general x10 -> x0, matrix products: 47.9 us -> none  [the longest x4 28.4 us: local(): jnp.einsum('ibjrtq,ijtqh->ibjrh', mixing, previous, preferred_element_typ...]
    all_to_all x1 -> x0, waiting for transfers between devices: 33.8 us -> none  [local(): lax.all_to_all(outgoing, 'leaf', split_axis=0, concat_axis=2, tiled=True)]
    transpose x4 -> x0, local copies, waits for them, and re-layouts: 28 us -> none  [the longest x3 28 us: local(): jnp.einsum('ibjrtq,ijtqh->ibjrh', mixing, previous, preferred_element_typ...]
    unnamed x32 -> x2, local copies, waits for them, and re-layouts: 28.5 us -> 2.96 us
    slice x1 -> x0, local copies, waits for them, and re-layouts: 11.4 us -> none  [local(): transfers[0, level_index - 1, 0]]
    gather x2 -> x0, local copies, waits for them, and re-layouts: 10.6 us -> none  [the longest x1 5.39 us: local(): jnp.take(incoming, inverse, axis=1).reshape(nodes_local, rank_width, sides)]
  transfers between devices with their start and end apart: 2 -> 0, of which waited for: 2 -> 0; matrix products, arithmetic and copies ran while one was open for 6% -> 0% of each run, Pallas kernels for 0% -> 0%
where the time goes in v1:
time: 97.5 us; the launch traced here: 97.3 us
  Pallas kernels  94.4 us (97%)
  local copies, waits for them, and re-layouts  2.96 us (3%)
    pallas_call x1, Pallas kernels, local(): pl.pallas_call(functools.partial(kernel, chunks, width, rank), out_shape=...  94.4 us
    unnamed x2, local copies, waits for them, and re-layouts  2.96 us

profile of v1, /device:TPU:0, one launch (start us, length us, event | category | flops | bytes accessed | tf_op | source)
XLA Modules:
  0.0 97.3 jit_solution(18061402343844500811)
XLA Ops:
  0.0 1.3 %copy.10 = s32[1,9,1,32]{3,1,2,0:T(8,128)} copy(s32[1,9,1,32]{3,2,1,0:T(1,128)} %param.11) | data formatting | bytes 2304
  1.3 94.4 %block_row.1 = bf16[256,512]{1,0:T(8,128)(2,1)} custom-call(bf16[32,128,512]{2,1,0:T(8,128)(2,1)} %bitcast.9, bf16[32,128,128]{2,1,0:T(8,128)(2,1)} %bitcast.11, bf16[8,32,128,256]{3,2,1,0:T(8,128)(2,1)} %bitcast.8, bf16[32,128,128]{2,1,0:T(8,128)(2,1)} %bitcast.12, s32[9,32]{1,0:T(8,128)} %bitcast.13, s32[8]{0:T(128)} %col_owner.1, s32[8]{0:T(128)} %row_owner.1), custom_call_target="tpu_custom_call" | custom-call | tf_op jit(solution)/shard_map/block_row/pallas_call | solution.py:328
  95.7 1.7 %copy.12 = bf16[1,256,512]{2,1,0:T(8,128)(2,1)} copy(bf16[1,256,512]{2,1,0:T(8,128)(2,1)} %bitcast.10) | data formatting | bytes 524288

commit v2 on v1

--- a/solution.py
+++ b/solution.py
@@ -18,7 +18,7 @@
 
 
 def kernel(
-    chunks, width, rank,
+    chunks, width, wide_width, rank,
     x_hbm, leaf_hbm, mix_hbm, row_hbm, ranks, col_owner, row_owner,
     out,
     xv, leaf, t1, t2, t3, t4, t5, t6, t7, t8, row,
@@ -41,10 +41,12 @@
     def z_peer(d):
         return {"blk": bx * SIDE + lax.rem(bz + d, SIDE), "leaf": me}
 
-    def x_in(c):
+    halves = wide_width // width
+
+    def x_in(w):
         return pltpu.make_async_copy(
-            x_hbm.at[:, :, pl.ds(pl.multiple_of(c * width, width), width)],
-            xv.at[c], x_sem.at[c])
+            x_hbm.at[:, :, pl.ds(pl.multiple_of(w * wide_width, wide_width), wide_width)],
+            xv.at[w], x_sem.at[w])
 
     def weight_in(i):
         if i == 0:
@@ -57,8 +59,8 @@
     x_in(0).start()
     for i in range(1, 5):
         weight_in(i).start()
-    for c in range(1, chunks):
-        x_in(c).start()
+    for w in range(1, chunks // halves):
+        x_in(w).start()
     for i in range(5, 10):
         weight_in(i).start()
 
@@ -69,9 +71,15 @@
         pl.semaphore_signal(barrier, inc=1, device_id=x_peer(d), device_id_type=MESH)
         pl.semaphore_signal(barrier, inc=1, device_id=z_peer(d), device_id_type=MESH)
 
-    row_ids = lax.broadcasted_iota(jnp.int32, (rank, width), 0)
+    places = []
+    for wanted in range(8):
+        found = jnp.int32(0)
+        for o in range(8):
+            found = found + jnp.where(col_owner[o] == wanted, o, 0)
+        places.append(lax.rem(me + 32 - found, 8))
 
     def keep(value, live):
+        row_ids = lax.broadcasted_iota(jnp.int32, value.shape, 0)
         return jnp.where(row_ids < live, value, 0.0).astype(jnp.bfloat16)
 
     def mix(lhs, top, bottom):
@@ -80,24 +88,24 @@
     def pair(ref, p):
         return ref[pl.ds(2 * p, 2)].reshape(2 * rank, 2 * rank)
 
-    def leaf_level(c):
-        @pl.loop(0, 8)
+    def leaf_level(w):
+        @pl.loop(0, 4)
         def _(g):
-            for u in range(4):
-                n = 4 * g + u
+            for u in range(8):
+                n = 8 * g + u
                 value = lax.dot_general(
-                    leaf[n], xv[c, n], (((0,), (0,)), ((), ())),
+                    leaf[n], xv[w, n], (((0,), (0,)), ((), ())),
                     preferred_element_type=jnp.float32)
                 ca[n] = keep(value, ranks[0, n])
 
     def column_level(level, source, target):
         half_i = 2 ** (level - 1)
 
-        @pl.loop(0, 4)
+        @pl.loop(0, 2)
         def _(g):
-            for u in range(4):
-                p = 4 * g + u
-                a = (p // half_i) * (2 * half_i) + p % half_i
+            for u in range(8):
+                p = 8 * g + u
+                a = 16 * g + (u // half_i) * (2 * half_i) + u % half_i
                 value = mix(pair(mixes[level - 1], p), source[a], source[a + half_i])
                 target[2 * p] = keep(value[:rank], ranks[level, 2 * p])
                 target[2 * p + 1] = keep(value[rank:], ranks[level, 2 * p + 1])
@@ -108,40 +116,45 @@
             send_sem=a_send.at[c, d - 1], recv_sem=a_recv.at[c, d - 1],
             device_id=leaf_peer(d), device_id_type=MESH)
 
-    def switch_level(c, source):
+    def switch_level(w, source):
         waiting = None
         for d in PEERS + (0,):
             s = row_owner[lax.rem(me + d, 8)]
             for j in range(2):
                 node = j * 8 + s
                 value = mix(pair(t4, node), source[2 * j * 8 + s], source[(2 * j + 1) * 8 + s])
-                send[c, d, j] = keep(value[:rank], ranks[4, 2 * node])
-                send[c, d, 2 + j] = keep(value[rank:], ranks[4, 2 * node + 1])
+                for e in range(2):
+                    kept = keep(value[e * rank:(e + 1) * rank], ranks[4, 2 * node + e])
+                    for h in range(halves):
+                        send[w * halves + h, d, 2 * e + j] = kept[:, h * width:(h + 1) * width]
             if waiting is not None:
-                a2a(c, waiting).start()
+                a2a(w * halves, waiting).start()
             waiting = d
-
-    def phase_a(c):
-        x_in(c).wait()
-
-        @pl.when(c == 0)
+        for h in range(1, halves):
+            for d in PEERS:
+                a2a(w * halves + h, d).start()
+
+    def phase_a(w):
+        x_in(w).wait()
+
+        @pl.when(w == 0)
         def _():
             weight_in(0).wait()
 
-        leaf_level(c)
+        leaf_level(w)
         for level, source, target in ((1, ca, cb), (2, cb, ca), (3, ca, cb)):
-            @pl.when(c == 0)
+            @pl.when(w == 0)
             def _():
                 weight_in(level).wait()
 
             column_level(level, source, target)
 
-        @pl.when(c == 0)
+        @pl.when(w == 0)
         def _():
             weight_in(4).wait()
             pl.semaphore_wait(barrier, 7 + 2 * (SIDE - 1))
 
-        switch_level(c, cb)
+        switch_level(w, cb)
 
     def x_first(c, d):
         return pltpu.make_async_remote_copy(
@@ -149,10 +162,10 @@
             send_sem=xs_sem.at[c, d - 1], recv_sem=xr_sem.at[c, d - 1],
             device_id=x_peer(d), device_id_type=MESH)
 
-    def z_first(c, d):
-        return pltpu.make_async_remote_copy(
-            src_ref=zs.at[c, d], dst_ref=zr.at[c, d - 1],
-            send_sem=zs_sem.at[c, d - 1], recv_sem=zr_sem.at[c, d - 1],
+    def z_first(c, d, half):
+        return pltpu.make_async_remote_copy(
+            src_ref=zs.at[c, d, pl.ds(2 * half, 2)], dst_ref=zr.at[c, d - 1, pl.ds(2 * half, 2)],
+            send_sem=zs_sem.at[c, d - 1, half], recv_sem=zr_sem.at[c, d - 1, half],
             device_id=z_peer(d), device_id_type=MESH)
 
     def z_second(c, d):
@@ -181,33 +194,44 @@
                 c5[2 * i + e, d] = keep(
                     value[e * rank:(e + 1) * rank], ranks[5, (2 * i + e) * 8 + j])
 
-    def quarter(c, dq, places):
-        q = lax.rem(bx + dq, SIDE)
-        for j in range(4):
-            lhs = jnp.concatenate([t6[2 * q * 4 + j], t6[(2 * q + 1) * 4 + j]], axis=0)
-            value = mix(lhs, c5[q, places[2 * j]], c5[q, places[2 * j + 1]])
-            for e in range(2):
-                c6[e * 4 + j] = keep(
-                    value[e * rank:(e + 1) * rank], ranks[6, (2 * q + e) * 4 + j])
-        for i in range(2):
-            for j in range(2):
-                base = (2 * q + i) * 4 + j
-                lhs = jnp.concatenate([t7[base], t7[base + 2]], axis=0)
-                value = mix(lhs, c6[i * 4 + 2 * j], c6[i * 4 + 2 * j + 1])
+    def quarters(c, half):
+        turns = tuple((k, dq, lax.rem(bx + dq, SIDE)) for k, dq in enumerate(QUARTERS[2 * half:2 * half + 2]))
+        for k, dq, q in turns:
+            for j in range(4):
+                lhs = jnp.concatenate([t6[2 * q * 4 + j], t6[(2 * q + 1) * 4 + j]], axis=0)
+                value = mix(lhs, c5[q, places[2 * j]], c5[q, places[2 * j + 1]])
                 for e in range(2):
-                    c7[(i * 2 + e) * 2 + j] = keep(
-                        value[e * rank:(e + 1) * rank], ranks[7, base + 2 * e])
-        for i in range(4):
-            node = 4 * q + i
-            value = mix(pair(t8, node), c7[2 * i], c7[2 * i + 1])
-            for e in range(2):
-                c8[2 * i + e] = keep(
-                    value[e * rank:(e + 1) * rank], ranks[8, 2 * node + e])
-        for m in range(4):
-            xs[c, dq, m] = dot(row[8 * q + 2 * m], c8[2 * m]).astype(jnp.bfloat16)
-        for r in range(SIDE):
-            m = lax.rem(bz + r, SIDE)
-            zs[c, r, dq] = dot(row[8 * q + 2 * m + 1], c8[2 * m + 1]).astype(jnp.bfloat16)
+                    c6[k, e * 4 + j] = keep(
+                        value[e * rank:(e + 1) * rank], ranks[6, (2 * q + e) * 4 + j])
+        for k, dq, q in turns:
+            for i in range(2):
+                for j in range(2):
+                    base = (2 * q + i) * 4 + j
+                    lhs = jnp.concatenate([t7[base], t7[base + 2]], axis=0)
+                    value = mix(lhs, c6[k, i * 4 + 2 * j], c6[k, i * 4 + 2 * j + 1])
+                    for e in range(2):
+                        c7[k, (i * 2 + e) * 2 + j] = keep(
+                            value[e * rank:(e + 1) * rank], ranks[7, base + 2 * e])
+        for k, dq, q in turns:
+            for i in range(4):
+                node = 4 * q + i
+                value = mix(pair(t8, node), c7[k, 2 * i], c7[k, 2 * i + 1])
+                for e in range(2):
+                    c8[k, 2 * i + e] = keep(
+                        value[e * rank:(e + 1) * rank], ranks[8, 2 * node + e])
+        for k, dq, q in turns:
+            for m in range(4):
+                xs[c, dq, m] = dot(row[8 * q + 2 * m], c8[k, 2 * m]).astype(jnp.bfloat16)
+        for k, dq, q in turns:
+            for r in range(SIDE):
+                m = lax.rem(bz + r, SIDE)
+                zs[c, r, 2 * half + k] = dot(
+                    row[8 * q + 2 * m + 1], c8[k, 2 * m + 1]).astype(jnp.bfloat16)
+        for k, dq, q in turns:
+            if dq:
+                x_first(c, dq).start()
+        for d in (2, 1, 3):
+            z_first(c, d, half).start()
 
     def phase_b(c):
         @pl.when(c == 0)
@@ -219,18 +243,8 @@
         for d in (7, 1, 6, 2, 5, 3, 4):
             a2a(c, d).wait_recv()
             arrive(c, d)
-        places = []
-        for wanted in range(8):
-            found = jnp.int32(0)
-            for o in range(8):
-                found = found + jnp.where(col_owner[o] == wanted, o, 0)
-            places.append(lax.rem(me + 32 - found, 8))
-        for index, dq in enumerate(QUARTERS):
-            quarter(c, dq, places)
-            if index:
-                x_first(c, QUARTERS[index - 1]).start()
-        for d in (2, 1, 3):
-            z_first(c, d).start()
+        quarters(c, 0)
+        quarters(c, 1)
 
     def wide(value):
         return value.astype(jnp.float32)
@@ -247,11 +261,13 @@
         for d in (2, 1, 3):
             z_second(c, d).start()
         for d in (2, 1, 3):
-            z_first(c, d).wait_recv()
+            for half in range(2):
+                z_first(c, d, half).wait_recv()
         for r in (2, 1, 3, 0):
-            total = wide(zs[c, 0, r])
+            slot = QUARTERS.index(r)
+            total = wide(zs[c, 0, slot])
             for d in range(SIDE - 1):
-                total = total + wide(zr[c, d, r])
+                total = total + wide(zr[c, d, slot])
             xs2[c, r] = total.astype(jnp.bfloat16)
         for d in (2, 1, 3):
             x_second(c, d).start()
@@ -271,9 +287,9 @@
             total = total + wide(xr2[c, d])
         out[pl.ds(rank, rank), columns] = total.astype(jnp.bfloat16)
 
-    @pl.loop(0, chunks)
-    def _(c):
-        phase_a(c)
+    @pl.loop(0, chunks // halves)
+    def _(w):
+        phase_a(w)
 
     @pl.loop(0, chunks)
     def _(c):
@@ -296,7 +312,8 @@
             a2a(c, d).wait_send()
         for d in range(1, SIDE):
             x_first(c, d).wait_send()
-            z_first(c, d).wait_send()
+            for half in range(2):
+                z_first(c, d, half).wait_send()
             x_second(c, d).wait_send()
             z_second(c, d).wait_send()
 
@@ -307,26 +324,27 @@
     levels = transfers.shape[1]
     width = 128
     chunks = sides // width
+    wide_width = 2 * width
     bf = jnp.bfloat16
     dma = pltpu.SemaphoreType.DMA
     hbm = pl.BlockSpec(memory_space=pltpu.HBM)
     smem = pl.BlockSpec(memory_space=pltpu.SMEM)
     tile = (rank, width)
-    scratch = [pltpu.VMEM((chunks, nodes, leaf_size, width), bf), pltpu.VMEM((nodes, leaf_size, rank), bf)]
+    scratch = [pltpu.VMEM((sides // wide_width, nodes, leaf_size, wide_width), bf), pltpu.VMEM((nodes, leaf_size, rank), bf)]
     scratch += [pltpu.VMEM((nodes, rank, 2 * rank), bf)] * levels
     scratch += [pltpu.VMEM((nodes, leaf_size, rank), bf)]
-    scratch += [pltpu.VMEM((nodes,) + tile, bf)] * 2
+    scratch += [pltpu.VMEM((nodes, rank, wide_width), bf)] * 2
     scratch += [pltpu.VMEM((chunks, 8, 4) + tile, bf), pltpu.VMEM((chunks, 7, 4) + tile, bf)]
-    scratch += [pltpu.VMEM((4, 8) + tile, bf)] + [pltpu.VMEM((8,) + tile, bf)] * 3
+    scratch += [pltpu.VMEM((4, 8) + tile, bf)] + [pltpu.VMEM((2, 8) + tile, bf)] * 3
     scratch += [pltpu.VMEM((chunks, 4, 4) + tile, bf)] * 2
     scratch += [pltpu.VMEM((chunks, 3, 4) + tile, bf)] * 2
     scratch += [pltpu.VMEM((chunks, 4) + tile, bf)] * 2
     scratch += [pltpu.VMEM((chunks, 3) + tile, bf)] * 2
-    scratch += [dma((10,)), dma((chunks,)), dma((chunks, 7)), dma((chunks, 7))]
-    scratch += [dma((chunks, 3))] * 8
+    scratch += [dma((10,)), dma((sides // wide_width,)), dma((chunks, 7)), dma((chunks, 7))]
+    scratch += [dma((chunks, 3))] * 2 + [dma((chunks, 3, 2))] * 2 + [dma((chunks, 3))] * 4
     share = nodes * leaf_size // lax.axis_size("blk")
     result = pl.pallas_call(
-        functools.partial(kernel, chunks, width, rank),
+        functools.partial(kernel, chunks, width, wide_width, rank),
         out_shape=jax.ShapeDtypeStruct((share, sides), bf),
         in_specs=[hbm] * 4 + [smem] * 3,
         out_specs=pl.BlockSpec(memory_space=pltpu.VMEM),

time: 97.5 us -> 83.2 us (0.85)
  Pallas kernels: 94.4 us -> 79.8 us
    pallas_call x1, Pallas kernels: 94.4 us -> 79.8 us  [local(): pl.pallas_call(functools.partial(kernel, chunks, width, wide_width, rank)...]
where the time goes in v2:
time: 83.2 us; the launch traced here: 82.8 us
  Pallas kernels  79.8 us (96%)
  local copies, waits for them, and re-layouts  2.96 us (4%)
    pallas_call x1, Pallas kernels, local(): pl.pallas_call(functools.partial(kernel, chunks, width, wide_width, rank)...  79.8 us
    unnamed x2, local copies, waits for them, and re-layouts  2.96 us

profile of v2, /device:TPU:0, one launch (start us, length us, event | category | flops | bytes accessed | tf_op | source)
XLA Modules:
  0.0 82.8 jit_solution(1234765165140774354)
XLA Ops:
  0.0 1.3 %copy.10 = s32[1,9,1,32]{3,1,2,0:T(8,128)} copy(s32[1,9,1,32]{3,2,1,0:T(1,128)} %param.11) | data formatting | bytes 2304
  1.3 79.8 %block_row.1 = bf16[256,512]{1,0:T(8,128)(2,1)} custom-call(bf16[32,128,512]{2,1,0:T(8,128)(2,1)} %bitcast.9, bf16[32,128,128]{2,1,0:T(8,128)(2,1)} %bitcast.11, bf16[8,32,128,256]{3,2,1,0:T(8,128)(2,1)} %bitcast.8, bf16[32,128,128]{2,1,0:T(8,128)(2,1)} %bitcast.12, s32[9,32]{1,0:T(8,128)} %bitcast.13, s32[8]{0:T(128)} %col_owner.1, s32[8]{0:T(128)} %row_owner.1), custom_call_target="tpu_custom_call" | custom-call | tf_op jit(solution)/shard_map/block_row/pallas_call | solution.py:346
  81.1 1.7 %copy.12 = bf16[1,256,512]{2,1,0:T(8,128)(2,1)} copy(bf16[1,256,512]{2,1,0:T(8,128)(2,1)} %bitcast.10) | data formatting | bytes 524288

commit v3 on v2

--- a/solution.py
+++ b/solution.py
@@ -10,7 +10,6 @@
 MESH = pl.DeviceIdType.MESH
 SIDE = 4
 PEERS = (4, 3, 5, 2, 6, 1, 7)
-QUARTERS = (2, 1, 3, 0)
 
 
 def dot(a, b):
@@ -32,6 +31,11 @@
     blk = lax.axis_index("blk")
     bx, bz = lax.div(blk, SIDE), lax.rem(blk, SIDE)
 
+    odd = lax.rem(bx, 2)
+    turns = ((2, 3 - 2 * odd), (1 + 2 * odd, 0))
+    x_pair = lax.div(bx, 2)
+    parts = (1 - x_pair, x_pair)
+
     def leaf_peer(d):
         return {"blk": blk, "leaf": lax.rem(me + d, 8)}
 
@@ -96,7 +100,7 @@
                 value = lax.dot_general(
                     leaf[n], xv[w, n], (((0,), (0,)), ((), ())),
                     preferred_element_type=jnp.float32)
-                ca[n] = keep(value, ranks[0, n])
+                ca[n] = keep(value, ranks[0, 0, 0, n])
 
     def column_level(level, source, target):
         half_i = 2 ** (level - 1)
@@ -107,13 +111,14 @@
                 p = 8 * g + u
                 a = 16 * g + (u // half_i) * (2 * half_i) + u % half_i
                 value = mix(pair(mixes[level - 1], p), source[a], source[a + half_i])
-                target[2 * p] = keep(value[:rank], ranks[level, 2 * p])
-                target[2 * p + 1] = keep(value[rank:], ranks[level, 2 * p + 1])
-
-    def a2a(c, d):
-        return pltpu.make_async_remote_copy(
-            src_ref=send.at[c, d], dst_ref=recv.at[c, d - 1],
-            send_sem=a_send.at[c, d - 1], recv_sem=a_recv.at[c, d - 1],
+                target[2 * p] = keep(value[:rank], ranks[0, level, 0, 2 * p])
+                target[2 * p + 1] = keep(value[rank:], ranks[0, level, 0, 2 * p + 1])
+
+    def a2a(c, d, half):
+        nodes = pl.ds(2 * parts[half], 2)
+        return pltpu.make_async_remote_copy(
+            src_ref=send.at[c, d, nodes], dst_ref=recv.at[c, d - 1, nodes],
+            send_sem=a_send.at[c, d - 1, half], recv_sem=a_recv.at[c, d - 1, half],
             device_id=leaf_peer(d), device_id_type=MESH)
 
     def switch_level(w, source):
@@ -124,15 +129,17 @@
                 node = j * 8 + s
                 value = mix(pair(t4, node), source[2 * j * 8 + s], source[(2 * j + 1) * 8 + s])
                 for e in range(2):
-                    kept = keep(value[e * rank:(e + 1) * rank], ranks[4, 2 * node + e])
+                    kept = keep(value[e * rank:(e + 1) * rank], ranks[0, 4, 0, 2 * node + e])
                     for h in range(halves):
                         send[w * halves + h, d, 2 * e + j] = kept[:, h * width:(h + 1) * width]
             if waiting is not None:
-                a2a(w * halves, waiting).start()
+                for half in range(2):
+                    a2a(w * halves, waiting, half).start()
             waiting = d
         for h in range(1, halves):
-            for d in PEERS:
-                a2a(w * halves + h, d).start()
+            for half in range(2):
+                for d in PEERS:
+                    a2a(w * halves + h, d, half).start()
 
     def phase_a(w):
         x_in(w).wait()
@@ -174,36 +181,37 @@
             send_sem=zs2_sem.at[c, d - 1], recv_sem=zr2_sem.at[c, d - 1],
             device_id=z_peer(d), device_id_type=MESH)
 
-    def x_second(c, d):
-        return pltpu.make_async_remote_copy(
-            src_ref=xs2.at[c, d], dst_ref=xr2.at[c, d - 1],
+    def x_second(c, slot):
+        d = turns[slot // 2][slot % 2]
+        return pltpu.make_async_remote_copy(
+            src_ref=xs2.at[c, slot], dst_ref=xr2.at[c, d - 1],
             send_sem=xs2_sem.at[c, d - 1], recv_sem=xr2_sem.at[c, d - 1],
             device_id=x_peer(d), device_id_type=MESH)
 
-    def arrive(c, d):
+    def arrive(c, d, half):
         owner = lax.rem(me + 8 - d, 8)
         j = col_owner[owner]
-        for i in range(2):
-            lhs = jnp.concatenate([t5[2 * i * 8 + j], t5[(2 * i + 1) * 8 + j]], axis=0)
-            if d == 0:
-                nodes = send[c, 0, pl.ds(2 * i, 2)]
-            else:
-                nodes = recv[c, d - 1, pl.ds(2 * i, 2)]
-            value = dot(lhs, nodes.reshape(2 * rank, width))
-            for e in range(2):
-                c5[2 * i + e, d] = keep(
-                    value[e * rank:(e + 1) * rank], ranks[5, (2 * i + e) * 8 + j])
+        i = parts[half]
+        lhs = jnp.concatenate([t5[2 * i * 8 + j], t5[(2 * i + 1) * 8 + j]], axis=0)
+        if d == 0:
+            nodes = send[c, 0, pl.ds(2 * i, 2)]
+        else:
+            nodes = recv[c, d - 1, pl.ds(2 * i, 2)]
+        value = dot(lhs, nodes.reshape(2 * rank, width))
+        for e in range(2):
+            c5[2 * i + e, d] = keep(
+                value[e * rank:(e + 1) * rank], ranks[0, 5, 0, (2 * i + e) * 8 + j])
 
     def quarters(c, half):
-        turns = tuple((k, dq, lax.rem(bx + dq, SIDE)) for k, dq in enumerate(QUARTERS[2 * half:2 * half + 2]))
-        for k, dq, q in turns:
+        pairs = tuple((k, dq, lax.rem(bx + dq, SIDE)) for k, dq in enumerate(turns[half]))
+        for k, dq, q in pairs:
             for j in range(4):
                 lhs = jnp.concatenate([t6[2 * q * 4 + j], t6[(2 * q + 1) * 4 + j]], axis=0)
                 value = mix(lhs, c5[q, places[2 * j]], c5[q, places[2 * j + 1]])
                 for e in range(2):
                     c6[k, e * 4 + j] = keep(
-                        value[e * rank:(e + 1) * rank], ranks[6, (2 * q + e) * 4 + j])
-        for k, dq, q in turns:
+                        value[e * rank:(e + 1) * rank], ranks[0, 6, 0, (2 * q + e) * 4 + j])
+        for k, dq, q in pairs:
             for i in range(2):
                 for j in range(2):
                     base = (2 * q + i) * 4 + j
@@ -211,24 +219,24 @@
                     value = mix(lhs, c6[k, i * 4 + 2 * j], c6[k, i * 4 + 2 * j + 1])
                     for e in range(2):
                         c7[k, (i * 2 + e) * 2 + j] = keep(
-                            value[e * rank:(e + 1) * rank], ranks[7, base + 2 * e])
-        for k, dq, q in turns:
+                            value[e * rank:(e + 1) * rank], ranks[0, 7, 0, base + 2 * e])
+        for k, dq, q in pairs:
             for i in range(4):
                 node = 4 * q + i
                 value = mix(pair(t8, node), c7[k, 2 * i], c7[k, 2 * i + 1])
                 for e in range(2):
                     c8[k, 2 * i + e] = keep(
-                        value[e * rank:(e + 1) * rank], ranks[8, 2 * node + e])
-        for k, dq, q in turns:
+                        value[e * rank:(e + 1) * rank], ranks[0, 8, 0, 2 * node + e])
+        for k, dq, q in pairs:
             for m in range(4):
                 xs[c, dq, m] = dot(row[8 * q + 2 * m], c8[k, 2 * m]).astype(jnp.bfloat16)
-        for k, dq, q in turns:
+        for k, dq, q in pairs:
             for r in range(SIDE):
                 m = lax.rem(bz + r, SIDE)
                 zs[c, r, 2 * half + k] = dot(
                     row[8 * q + 2 * m + 1], c8[k, 2 * m + 1]).astype(jnp.bfloat16)
-        for k, dq, q in turns:
-            if dq:
+        for k, dq, q in pairs:
+            if half == 0 or k == 0:
                 x_first(c, dq).start()
         for d in (2, 1, 3):
             z_first(c, d, half).start()
@@ -239,12 +247,16 @@
             for i in range(5, 10):
                 weight_in(i).wait()
 
-        arrive(c, 0)
-        for d in (7, 1, 6, 2, 5, 3, 4):
-            a2a(c, d).wait_recv()
-            arrive(c, d)
-        quarters(c, 0)
-        quarters(c, 1)
+        for half in range(2):
+            arrive(c, 0, half)
+            for d in (7, 1, 6, 2, 5, 3, 4):
+                a2a(c, d, half).wait_recv()
+                arrive(c, d, half)
+            quarters(c, half)
+            if half == 0:
+                @pl.when(c >= 1)
+                def _():
+                    first_sum(c - 1)
 
     def wide(value):
         return value.astype(jnp.float32)
@@ -263,14 +275,13 @@
         for d in (2, 1, 3):
             for half in range(2):
                 z_first(c, d, half).wait_recv()
-        for r in (2, 1, 3, 0):
-            slot = QUARTERS.index(r)
+        for slot in range(SIDE):
             total = wide(zs[c, 0, slot])
             for d in range(SIDE - 1):
                 total = total + wide(zr[c, d, slot])
-            xs2[c, r] = total.astype(jnp.bfloat16)
-        for d in (2, 1, 3):
-            x_second(c, d).start()
+            xs2[c, slot] = total.astype(jnp.bfloat16)
+        for slot in range(SIDE - 1):
+            x_second(c, slot).start()
 
     def last_sum(c):
         columns = pl.ds(pl.multiple_of(c * width, width), width)
@@ -280,9 +291,9 @@
         for d in range(SIDE - 1):
             total = total + wide(zr2[c, d])
         out[pl.ds(0, rank), columns] = total.astype(jnp.bfloat16)
-        for d in (1, 3, 2):
-            x_second(c, d).wait_recv()
-        total = wide(xs2[c, 0])
+        for slot in range(SIDE - 1):
+            x_second(c, slot).wait_recv()
+        total = wide(xs2[c, SIDE - 1])
         for d in range(SIDE - 1):
             total = total + wide(xr2[c, d])
         out[pl.ds(rank, rank), columns] = total.astype(jnp.bfloat16)
@@ -293,10 +304,6 @@
 
     @pl.loop(0, chunks)
     def _(c):
-        @pl.when(c >= 1)
-        def _():
-            first_sum(c - 1)
-
         phase_b(c)
 
         @pl.when(c >= 1)
@@ -309,12 +316,13 @@
     @pl.loop(0, chunks)
     def _(c):
         for d in range(1, 8):
-            a2a(c, d).wait_send()
+            for half in range(2):
+                a2a(c, d, half).wait_send()
         for d in range(1, SIDE):
             x_first(c, d).wait_send()
             for half in range(2):
                 z_first(c, d, half).wait_send()
-            x_second(c, d).wait_send()
+            x_second(c, d - 1).wait_send()
             z_second(c, d).wait_send()
 
 
@@ -340,7 +348,7 @@
     scratch += [pltpu.VMEM((chunks, 3, 4) + tile, bf)] * 2
     scratch += [pltpu.VMEM((chunks, 4) + tile, bf)] * 2
     scratch += [pltpu.VMEM((chunks, 3) + tile, bf)] * 2
-    scratch += [dma((10,)), dma((sides // wide_width,)), dma((chunks, 7)), dma((chunks, 7))]
+    scratch += [dma((10,)), dma((sides // wide_width,)), dma((chunks, 7, 2)), dma((chunks, 7, 2))]
     scratch += [dma((chunks, 3))] * 2 + [dma((chunks, 3, 2))] * 2 + [dma((chunks, 3))] * 4
     share = nodes * leaf_size // lax.axis_size("blk")
     result = pl.pallas_call(
@@ -357,7 +365,7 @@
         leaf_basis[0, 0],
         transfers[0, :, 0],
         row_basis[0, 0],
-        ranks[0, :, 0],
+        ranks,
         col_owner,
         row_owner,
     )

time: 83.2 us -> 82.9 us (level)
  local copies, waits for them, and re-layouts: 2.96 us -> 1.67 us
  Pallas kernels: 79.8 us -> 80.8 us
    unnamed x2 -> x1, local copies, waits for them, and re-layouts: 2.96 us -> 1.67 us
    pallas_call x1, Pallas kernels: 79.8 us -> 80.8 us  [local(): pl.pallas_call(functools.partial(kernel, chunks, width, wide_width, rank)...]
where the time goes in v3:
time: 82.9 us; the launch traced here: 82.5 us
  Pallas kernels  80.8 us (97%)
  local copies, waits for them, and re-layouts  1.67 us (2%)
    pallas_call x1, Pallas kernels, local(): pl.pallas_call(functools.partial(kernel, chunks, width, wide_width, rank)...  80.8 us
    unnamed x1, local copies, waits for them, and re-layouts  1.67 us

profile of v3, /device:TPU:0, one launch (start us, length us, event | category | flops | bytes accessed | tf_op | source)
XLA Modules:
  0.0 82.5 jit_solution(10248798791596139944)
XLA Ops:
  0.0 80.8 %block_row.1 = bf16[256,512]{1,0:T(8,128)(2,1)} custom-call(bf16[32,128,512]{2,1,0:T(8,128)(2,1)} %bitcast.6, bf16[32,128,128]{2,1,0:T(8,128)(2,1)} %bitcast.8, bf16[8,32,128,256]{3,2,1,0:T(8,128)(2,1)} %bitcast.5, bf16[32,128,128]{2,1,0:T(8,128)(2,1)} %bitcast.9, s32[1,9,1,32]{3,2,1,0:T(1,128)} %ranks.1, s32[8]{0:T(128)} %col_owner.1, s32[8]{0:T(128)} %row_owner.1), custom_call_target="tpu_custom_call" | custom-call | tf_op jit(solution)/shard_map/block_row/pallas_call | solution.py:354
  80.8 1.7 %copy.9 = bf16[1,256,512]{2,1,0:T(8,128)(2,1)} copy(bf16[1,256,512]{2,1,0:T(8,128)(2,1)} %bitcast.7) | data formatting | bytes 524288

commit v4 on v3

--- a/solution.py
+++ b/solution.py
@@ -10,6 +10,8 @@
 MESH = pl.DeviceIdType.MESH
 SIDE = 4
 PEERS = (4, 3, 5, 2, 6, 1, 7)
+ARRIVALS = (7, 1, 6, 2, 5, 3, 4)
+AHEAD = 12
 
 
 def dot(a, b):
@@ -61,12 +63,6 @@
 
     weight_in(0).start()
     x_in(0).start()
-    for i in range(1, 5):
-        weight_in(i).start()
-    for w in range(1, chunks // halves):
-        x_in(w).start()
-    for i in range(5, 10):
-        weight_in(i).start()
 
     barrier = pltpu.get_barrier_semaphore()
     for d in range(1, 8):
@@ -133,13 +129,16 @@
                     for h in range(halves):
                         send[w * halves + h, d, 2 * e + j] = kept[:, h * width:(h + 1) * width]
             if waiting is not None:
-                for half in range(2):
-                    a2a(w * halves, waiting, half).start()
+                @pl.when(w == 0)
+                def _():
+                    a2a(0, waiting, 0).start()
+
             waiting = d
-        for h in range(1, halves):
-            for half in range(2):
-                for d in PEERS:
-                    a2a(w * halves + h, d, half).start()
+
+        @pl.when(w == 0)
+        def _():
+            for d in ARRIVALS[:AHEAD - 7]:
+                a2a(0, d, 1).start()
 
     def phase_a(w):
         x_in(w).wait()
@@ -147,21 +146,37 @@
         @pl.when(w == 0)
         def _():
             weight_in(0).wait()
+            weight_in(2).start()
+            weight_in(3).start()
 
         leaf_level(w)
         for level, source, target in ((1, ca, cb), (2, cb, ca), (3, ca, cb)):
             @pl.when(w == 0)
             def _():
                 weight_in(level).wait()
+                if level == 1:
+                    weight_in(4).start()
 
             column_level(level, source, target)
 
         @pl.when(w == 0)
         def _():
             weight_in(4).wait()
+            for later in range(1, chunks // halves):
+                x_in(later).start()
+            for i in range(5, 10):
+                weight_in(i).start()
             pl.semaphore_wait(barrier, 7 + 2 * (SIDE - 1))
 
         switch_level(w, cb)
+
+    def follow(c, unit, d):
+        if unit < 2:
+            a2a(c, d, unit).start()
+        else:
+            @pl.when(c + unit // 2 < chunks)
+            def _():
+                a2a(c + unit // 2, d, unit % 2).start()
 
     def x_first(c, d):
         return pltpu.make_async_remote_copy(
@@ -249,8 +264,9 @@
 
         for half in range(2):
             arrive(c, 0, half)
-            for d in (7, 1, 6, 2, 5, 3, 4):
+            for k, d in enumerate(ARRIVALS):
                 a2a(c, d, half).wait_recv()
+                follow(c, half + (k + AHEAD) // 7, ARRIVALS[(k + AHEAD) % 7])
                 arrive(c, d, half)
             quarters(c, half)
             if half == 0:
@@ -297,6 +313,8 @@
         for d in range(SIDE - 1):
             total = total + wide(xr2[c, d])
         out[pl.ds(rank, rank), columns] = total.astype(jnp.bfloat16)
+
+    weight_in(1).start()
 
     @pl.loop(0, chunks // halves)
     def _(w):

time: 82.9 us -> 76.7 us (0.925)
  Pallas kernels: 80.8 us -> 74.7 us
    pallas_call x1, Pallas kernels: 80.8 us -> 74.7 us  [local(): pl.pallas_call(functools.partial(kernel, chunks, width, wide_width, rank)...]
where the time goes in v4:
time: 76.7 us; the launch traced here: 76.4 us
  Pallas kernels  74.7 us (97%)
  local copies, waits for them, and re-layouts  1.67 us (2%)
    pallas_call x1, Pallas kernels, local(): pl.pallas_call(functools.partial(kernel, chunks, width, wide_width, rank)...  74.7 us
    unnamed x1, local copies, waits for them, and re-layouts  1.67 us

profile of v4, /device:TPU:0, one launch (start us, length us, event | category | flops | bytes accessed | tf_op | source)
XLA Modules:
  0.0 76.4 jit_solution(10006175736390903984)
XLA Ops:
  0.0 74.7 %block_row.1 = bf16[256,512]{1,0:T(8,128)(2,1)} custom-call(bf16[32,128,512]{2,1,0:T(8,128)(2,1)} %bitcast.6, bf16[32,128,128]{2,1,0:T(8,128)(2,1)} %bitcast.8, bf16[8,32,128,256]{3,2,1,0:T(8,128)(2,1)} %bitcast.5, bf16[32,128,128]{2,1,0:T(8,128)(2,1)} %bitcast.9, s32[1,9,1,32]{3,2,1,0:T(1,128)} %ranks.1, s32[8]{0:T(128)} %col_owner.1, s32[8]{0:T(128)} %row_owner.1), custom_call_target="tpu_custom_call" | custom-call | tf_op jit(solution)/shard_map/block_row/pallas_call | solution.py:372
  74.7 1.7 %copy.9 = bf16[1,256,512]{2,1,0:T(8,128)(2,1)} copy(bf16[1,256,512]{2,1,0:T(8,128)(2,1)} %bitcast.7) | data formatting | bytes 524288

commit v5 on v4

--- a/solution.py
+++ b/solution.py
@@ -11,7 +11,7 @@
 SIDE = 4
 PEERS = (4, 3, 5, 2, 6, 1, 7)
 ARRIVALS = (7, 1, 6, 2, 5, 3, 4)
-AHEAD = 12
+AHEAD = 14
 
 
 def dot(a, b):
@@ -19,11 +19,11 @@
 
 
 def kernel(
-    chunks, width, wide_width, rank,
+    chunks, width, rank,
     x_hbm, leaf_hbm, mix_hbm, row_hbm, ranks, col_owner, row_owner,
     out,
-    xv, leaf, t1, t2, t3, t4, t5, t6, t7, t8, row,
-    ca, cb, send, recv, c5, c6, c7, c8,
+    x_head, x_tail, leaf, t1, t2, t3, t4, t5, t6, t7, t8, row,
+    head_a, head_b, tail_a, tail_b, send, recv, c5, c6, c7, c8,
     xs, zs, xr, zr, xs2, zs2, xr2, zr2,
     in_sem, x_sem,
     a_send, a_recv, xs_sem, xr_sem, zs_sem, zr_sem, xs2_sem, xr2_sem, zs2_sem, zr2_sem,
@@ -47,12 +47,11 @@
     def z_peer(d):
         return {"blk": bx * SIDE + lax.rem(bz + d, SIDE), "leaf": me}
 
-    halves = wide_width // width
-
-    def x_in(w):
+    def x_in(tail):
+        first, count = (1, chunks - 1) if tail else (0, 1)
         return pltpu.make_async_copy(
-            x_hbm.at[:, :, pl.ds(pl.multiple_of(w * wide_width, wide_width), wide_width)],
-            xv.at[w], x_sem.at[w])
+            x_hbm.at[:, :, pl.ds(first * width, count * width)],
+            x_tail if tail else x_head, x_sem.at[int(tail)])
 
     def weight_in(i):
         if i == 0:
@@ -62,7 +61,7 @@
         return pltpu.make_async_copy(mix_hbm.at[i - 1], mixes[i - 1], in_sem.at[i])
 
     weight_in(0).start()
-    x_in(0).start()
+    x_in(False).start()
 
     barrier = pltpu.get_barrier_semaphore()
     for d in range(1, 8):
@@ -88,15 +87,15 @@
     def pair(ref, p):
         return ref[pl.ds(2 * p, 2)].reshape(2 * rank, 2 * rank)
 
-    def leaf_level(w):
+    def leaf_level(source, target):
         @pl.loop(0, 4)
         def _(g):
             for u in range(8):
                 n = 8 * g + u
                 value = lax.dot_general(
-                    leaf[n], xv[w, n], (((0,), (0,)), ((), ())),
+                    leaf[n], source[n], (((0,), (0,)), ((), ())),
                     preferred_element_type=jnp.float32)
-                ca[n] = keep(value, ranks[0, 0, 0, n])
+                target[n] = keep(value, ranks[0, 0, 0, n])
 
     def column_level(level, source, target):
         half_i = 2 ** (level - 1)
@@ -117,7 +116,8 @@
             send_sem=a_send.at[c, d - 1, half], recv_sem=a_recv.at[c, d - 1, half],
             device_id=leaf_peer(d), device_id_type=MESH)
 
-    def switch_level(w, source):
+    def switch_level(tail, source):
+        first, count = (1, chunks - 1) if tail else (0, 1)
         waiting = None
         for d in PEERS + (0,):
             s = row_owner[lax.rem(me + d, 8)]
@@ -126,49 +126,36 @@
                 value = mix(pair(t4, node), source[2 * j * 8 + s], source[(2 * j + 1) * 8 + s])
                 for e in range(2):
                     kept = keep(value[e * rank:(e + 1) * rank], ranks[0, 4, 0, 2 * node + e])
-                    for h in range(halves):
-                        send[w * halves + h, d, 2 * e + j] = kept[:, h * width:(h + 1) * width]
-            if waiting is not None:
-                @pl.when(w == 0)
-                def _():
-                    a2a(0, waiting, 0).start()
-
+                    for h in range(count):
+                        send[first + h, d, 2 * e + j] = kept[:, h * width:(h + 1) * width]
+            if waiting is not None and not tail:
+                a2a(0, waiting, 0).start()
             waiting = d
-
-        @pl.when(w == 0)
-        def _():
+        if not tail:
             for d in ARRIVALS[:AHEAD - 7]:
                 a2a(0, d, 1).start()
 
-    def phase_a(w):
-        x_in(w).wait()
-
-        @pl.when(w == 0)
-        def _():
+    def phase_a(tail):
+        even, odd_levels = (tail_a, tail_b) if tail else (head_a, head_b)
+        x_in(tail).wait()
+        if not tail:
             weight_in(0).wait()
             weight_in(2).start()
             weight_in(3).start()
-
-        leaf_level(w)
-        for level, source, target in ((1, ca, cb), (2, cb, ca), (3, ca, cb)):
-            @pl.when(w == 0)
-            def _():
+        leaf_level(x_tail if tail else x_head, even)
+        for level, source, target in ((1, even, odd_levels), (2, odd_levels, even), (3, even, odd_levels)):
+            if not tail:
                 weight_in(level).wait()
                 if level == 1:
                     weight_in(4).start()
-
             column_level(level, source, target)
-
-        @pl.when(w == 0)
-        def _():
+        if not tail:
             weight_in(4).wait()
-            for later in range(1, chunks // halves):
-                x_in(later).start()
+            x_in(True).start()
             for i in range(5, 10):
                 weight_in(i).start()
             pl.semaphore_wait(barrier, 7 + 2 * (SIDE - 1))
-
-        switch_level(w, cb)
+        switch_level(tail, odd_levels)
 
     def follow(c, unit, d):
         if unit < 2:
@@ -250,7 +237,6 @@
                 m = lax.rem(bz + r, SIDE)
                 zs[c, r, 2 * half + k] = dot(
                     row[8 * q + 2 * m + 1], c8[k, 2 * m + 1]).astype(jnp.bfloat16)
-        for k, dq, q in pairs:
             if half == 0 or k == 0:
                 x_first(c, dq).start()
         for d in (2, 1, 3):
@@ -277,27 +263,41 @@
     def wide(value):
         return value.astype(jnp.float32)
 
+    def x_total(c, m):
+        total = wide(xs[c, 0, m])
+        for d in range(SIDE - 1):
+            total = total + wide(xr[c, d, m])
+        return total.astype(jnp.bfloat16)
+
+    def z_total(c, slot):
+        total = wide(zs[c, 0, slot])
+        for d in range(SIDE - 1):
+            total = total + wide(zr[c, d, slot])
+        return total.astype(jnp.bfloat16)
+
     def first_sum(c):
         for d in (2, 1, 3):
+            z_first(c, d, 0).wait_recv()
+        for slot in range(2):
+            xs2[c, slot] = z_total(c, slot)
+        for d in (2, 1, 3):
             x_first(c, d).wait_recv()
-        for r in (2, 1, 3, 0):
-            m = lax.rem(bz + r, SIDE)
-            total = wide(xs[c, 0, m])
-            for d in range(SIDE - 1):
-                total = total + wide(xr[c, d, m])
-            zs2[c, r] = total.astype(jnp.bfloat16)
+        ready = None
+        for r in (2, 1, 3):
+            zs2[c, r] = x_total(c, lax.rem(bz + r, SIDE))
+            if ready is None:
+                for slot in range(2):
+                    x_second(c, slot).start()
+            else:
+                z_second(c, ready).start()
+            ready = r
         for d in (2, 1, 3):
-            z_second(c, d).start()
-        for d in (2, 1, 3):
-            for half in range(2):
-                z_first(c, d, half).wait_recv()
-        for slot in range(SIDE):
-            total = wide(zs[c, 0, slot])
-            for d in range(SIDE - 1):
-                total = total + wide(zr[c, d, slot])
-            xs2[c, slot] = total.astype(jnp.bfloat16)
-        for slot in range(SIDE - 1):
-            x_second(c, slot).start()
+            z_first(c, d, 1).wait_recv()
+        xs2[c, 2] = z_total(c, 2)
+        z_second(c, ready).start()
+        zs2[c, 0] = x_total(c, bz)
+        x_second(c, 2).start()
+        xs2[c, 3] = z_total(c, 3)
 
     def last_sum(c):
         columns = pl.ds(pl.multiple_of(c * width, width), width)
@@ -316,9 +316,8 @@
 
     weight_in(1).start()
 
-    @pl.loop(0, chunks // halves)
-    def _(w):
-        phase_a(w)
+    phase_a(False)
+    phase_a(True)
 
     @pl.loop(0, chunks)
     def _(c):
@@ -350,27 +349,28 @@
     levels = transfers.shape[1]
     width = 128
     chunks = sides // width
-    wide_width = 2 * width
+    rest = sides - width
     bf = jnp.bfloat16
     dma = pltpu.SemaphoreType.DMA
     hbm = pl.BlockSpec(memory_space=pltpu.HBM)
     smem = pl.BlockSpec(memory_space=pltpu.SMEM)
     tile = (rank, width)
-    scratch = [pltpu.VMEM((sides // wide_width, nodes, leaf_size, wide_width), bf), pltpu.VMEM((nodes, leaf_size, rank), bf)]
+    scratch = [pltpu.VMEM((nodes, leaf_size, width), bf), pltpu.VMEM((nodes, leaf_size, rest), bf)]
+    scratch += [pltpu.VMEM((nodes, leaf_size, rank), bf)]
     scratch += [pltpu.VMEM((nodes, rank, 2 * rank), bf)] * levels
     scratch += [pltpu.VMEM((nodes, leaf_size, rank), bf)]
-    scratch += [pltpu.VMEM((nodes, rank, wide_width), bf)] * 2
+    scratch += [pltpu.VMEM((nodes, rank, width), bf)] * 2 + [pltpu.VMEM((nodes, rank, rest), bf)] * 2
     scratch += [pltpu.VMEM((chunks, 8, 4) + tile, bf), pltpu.VMEM((chunks, 7, 4) + tile, bf)]
     scratch += [pltpu.VMEM((4, 8) + tile, bf)] + [pltpu.VMEM((2, 8) + tile, bf)] * 3
     scratch += [pltpu.VMEM((chunks, 4, 4) + tile, bf)] * 2
     scratch += [pltpu.VMEM((chunks, 3, 4) + tile, bf)] * 2
     scratch += [pltpu.VMEM((chunks, 4) + tile, bf)] * 2
     scratch += [pltpu.VMEM((chunks, 3) + tile, bf)] * 2
-    scratch += [dma((10,)), dma((sides // wide_width,)), dma((chunks, 7, 2)), dma((chunks, 7, 2))]
+    scratch += [dma((10,)), dma((2,)), dma((chunks, 7, 2)), dma((chunks, 7, 2))]
     scratch += [dma((chunks, 3))] * 2 + [dma((chunks, 3, 2))] * 2 + [dma((chunks, 3))] * 4
     share = nodes * leaf_size // lax.axis_size("blk")
     result = pl.pallas_call(
-        functools.partial(kernel, chunks, width, wide_width, rank),
+        functools.partial(kernel, chunks, width, rank),
         out_shape=jax.ShapeDtypeStruct((share, sides), bf),
         in_specs=[hbm] * 4 + [smem] * 3,
         out_specs=pl.BlockSpec(memory_space=pltpu.VMEM),

time: 76.7 us -> 73.2 us (0.954)
  Pallas kernels: 74.7 us -> 71.3 us
    pallas_call x1, Pallas kernels: 74.7 us -> 71.3 us  [local(): pl.pallas_call(functools.partial(kernel, chunks, width, rank), out_shape=...]
where the time goes in v5:
time: 73.2 us; the launch traced here: 73 us
  Pallas kernels  71.3 us (97%)
  local copies, waits for them, and re-layouts  1.67 us (2%)
    pallas_call x1, Pallas kernels, local(): pl.pallas_call(functools.partial(kernel, chunks, width, rank), out_shape=...  71.3 us
    unnamed x1, local copies, waits for them, and re-layouts  1.67 us

profile of v5, /device:TPU:0, one launch (start us, length us, event | category | flops | bytes accessed | tf_op | source)
XLA Modules:
  0.0 73.0 jit_solution(13947847627018101586)
XLA Ops:
  0.0 71.3 %block_row.1 = bf16[256,512]{1,0:T(8,128)(2,1)} custom-call(bf16[32,128,512]{2,1,0:T(8,128)(2,1)} %bitcast.6, bf16[32,128,128]{2,1,0:T(8,128)(2,1)} %bitcast.8, bf16[8,32,128,256]{3,2,1,0:T(8,128)(2,1)} %bitcast.5, bf16[32,128,128]{2,1,0:T(8,128)(2,1)} %bitcast.9, s32[1,9,1,32]{3,2,1,0:T(1,128)} %ranks.1, s32[8]{0:T(128)} %col_owner.1, s32[8]{0:T(128)} %row_owner.1), custom_call_target="tpu_custom_call" | custom-call | tf_op jit(solution)/shard_map/block_row/pallas_call | solution.py:372
  71.3 1.7 %copy.9 = bf16[1,256,512]{2,1,0:T(8,128)(2,1)} copy(bf16[1,256,512]{2,1,0:T(8,128)(2,1)} %bitcast.7) | data formatting | bytes 524288

commit v6 on v5

--- a/solution.py
+++ b/solution.py
@@ -256,7 +256,7 @@
                 arrive(c, d, half)
             quarters(c, half)
             if half == 0:
-                @pl.when(c >= 1)
+                @pl.when(c == chunks - 1)
                 def _():
                     first_sum(c - 1)
 
@@ -316,22 +316,7 @@
 
     weight_in(1).start()
 
-    phase_a(False)
-    phase_a(True)
-
-    @pl.loop(0, chunks)
-    def _(c):
-        phase_b(c)
-
-        @pl.when(c >= 1)
-        def _():
-            last_sum(c - 1)
-
-    first_sum(chunks - 1)
-    last_sum(chunks - 1)
-
-    @pl.loop(0, chunks)
-    def _(c):
+    def drain(c):
         for d in range(1, 8):
             for half in range(2):
                 a2a(c, d, half).wait_send()
@@ -341,6 +326,32 @@
                 z_first(c, d, half).wait_send()
             x_second(c, d - 1).wait_send()
             z_second(c, d).wait_send()
+
+    phase_a(False)
+    phase_a(True)
+
+    @pl.loop(0, chunks)
+    def _(c):
+        phase_b(c)
+
+        @pl.when((c >= 1) & (c < chunks - 1))
+        def _():
+            first_sum(c - 1)
+
+        @pl.when(c >= 2)
+        def _():
+            last_sum(c - 2)
+
+    first_sum(chunks - 1)
+    last_sum(chunks - 2)
+
+    @pl.loop(0, chunks - 1)
+    def _(c):
+        drain(c)
+
+    last_sum(chunks - 1)
+
+    drain(chunks - 1)
 
 
 def local(columns_in, leaf_basis, transfers, row_basis, ranks, col_owner, row_owner):

time: 73.2 us -> 72.5 us (level)
  no operation moved by 1% of the time
where the time goes in v6:
time: 72.5 us; the launch traced here: 72.4 us
  Pallas kernels  70.7 us (98%)
  local copies, waits for them, and re-layouts  1.67 us (2%)
    pallas_call x1, Pallas kernels, local(): pl.pallas_call(functools.partial(kernel, chunks, width, rank), out_shape=...  70.7 us
    unnamed x1, local copies, waits for them, and re-layouts  1.67 us

profile of v6, /device:TPU:0, one launch (start us, length us, event | category | flops | bytes accessed | tf_op | source)
XLA Modules:
  0.0 72.4 jit_solution(4213023128052233696)
XLA Ops:
  0.0 70.7 %block_row.1 = bf16[256,512]{1,0:T(8,128)(2,1)} custom-call(bf16[32,128,512]{2,1,0:T(8,128)(2,1)} %bitcast.6, bf16[32,128,128]{2,1,0:T(8,128)(2,1)} %bitcast.8, bf16[8,32,128,256]{3,2,1,0:T(8,128)(2,1)} %bitcast.5, bf16[32,128,128]{2,1,0:T(8,128)(2,1)} %bitcast.9, s32[1,9,1,32]{3,2,1,0:T(1,128)} %ranks.1, s32[8]{0:T(128)} %col_owner.1, s32[8]{0:T(128)} %row_owner.1), custom_call_target="tpu_custom_call" | custom-call | tf_op jit(solution)/shard_map/block_row/pallas_call | solution.py:383
  70.7 1.7 %copy.9 = bf16[1,256,512]{2,1,0:T(8,128)(2,1)} copy(bf16[1,256,512]{2,1,0:T(8,128)(2,1)} %bitcast.7) | data formatting | bytes 524288

commit v7 on v6

--- a/solution.py
+++ b/solution.py
@@ -237,8 +237,8 @@
                 m = lax.rem(bz + r, SIDE)
                 zs[c, r, 2 * half + k] = dot(
                     row[8 * q + 2 * m + 1], c8[k, 2 * m + 1]).astype(jnp.bfloat16)
-            if half == 0 or k == 0:
-                x_first(c, dq).start()
+                if r == 0 and (half == 0 or k == 0):
+                    x_first(c, dq).start()
         for d in (2, 1, 3):
             z_first(c, d, half).start()
 

time: 72.5 us -> 72.5 us (level)
  no operation moved by 1% of the time
where the time goes in v7:
time: 72.5 us; the launch traced here: 72.3 us
  Pallas kernels  70.6 us (97%)
  local copies, waits for them, and re-layouts  1.67 us (2%)
    pallas_call x1, Pallas kernels, local(): pl.pallas_call(functools.partial(kernel, chunks, width, rank), out_shape=...  70.6 us
    unnamed x1, local copies, waits for them, and re-layouts  1.67 us

profile of v7, /device:TPU:0, one launch (start us, length us, event | category | flops | bytes accessed | tf_op | source)
XLA Modules:
  0.0 72.3 jit_solution(872877223138811685)
XLA Ops:
  0.0 70.6 %block_row.1 = bf16[256,512]{1,0:T(8,128)(2,1)} custom-call(bf16[32,128,512]{2,1,0:T(8,128)(2,1)} %bitcast.6, bf16[32,128,128]{2,1,0:T(8,128)(2,1)} %bitcast.8, bf16[8,32,128,256]{3,2,1,0:T(8,128)(2,1)} %bitcast.5, bf16[32,128,128]{2,1,0:T(8,128)(2,1)} %bitcast.9, s32[1,9,1,32]{3,2,1,0:T(1,128)} %ranks.1, s32[8]{0:T(128)} %col_owner.1, s32[8]{0:T(128)} %row_owner.1), custom_call_target="tpu_custom_call" | custom-call | tf_op jit(solution)/shard_map/block_row/pallas_call | solution.py:383
  70.6 1.7 %copy.9 = bf16[1,256,512]{2,1,0:T(8,128)(2,1)} copy(bf16[1,256,512]{2,1,0:T(8,128)(2,1)} %bitcast.7) | data formatting | bytes 524288
